TPU v7x, 32 devices: a whole 2x2x4 slice. The times are simulated.
32 devices in a mesh: gx: 2 (over y), gy: 4 (over x, core), shot: 4 (over z).
Axes of the slice: x: 2, y: 2, z: 4, core: 2. Of those that a mesh axis runs over, the one named last changes fastest.
Arguments:
- adj_prev: float32 [4, 64, 64, 256], P('shot', 'gx', 'gy'), may hold values from -6 to 6
- adj_cur: float32 [4, 64, 64, 256], P('shot', 'gx', 'gy'), may hold values from -6 to 6
- fwd_accel: bfloat16 [4, 4, 64, 64, 256], P('shot', None, 'gx', 'gy'), may hold values from -6 to 6
- courant2: float32 [64, 64, 256], P('gx', 'gy'), may hold values from 0.05 to 0.18
- traces: bfloat16 [4, 4, 512], P('shot', None, ('gx', 'gy')), may hold values from -6 to 6
- weights: bfloat16 [2, 4, 64, 16, 256], P('gx', 'gy'), may hold values from -3 to 3
- rblock: int32 [2, 4, 64], P('gx', 'gy'), may hold values from 0 to 31
- column: int32 [2, 4, 64], P('gx', 'gy'), may hold values from 0 to 511
- counts: int32 [2, 4], P('gx', 'gy'), may hold values from 16 to 64
Outputs:
- adj_prev_out: float32 [4, 64, 64, 256], P('shot', 'gx', 'gy')
- adj_cur_out: float32 [4, 64, 64, 256], P('shot', 'gx', 'gy')
- gradient: float32 [32, 32, 128], P('gx', 'gy')
All inputs are finite; a program needn't handle non-finite values.
Results may differ from a plain program's by a relative error of at most 0.00045.
Values may be sent and summed in bfloat16 or wider, within the bound.
No kernel may reach another device: no remote copies, remote signals or barrier semaphores. Data moves between devices by JAX's collectives and lax.ppermute only.
A program may use at most 128 MiB of HBM per device.

v0:
```python
import jax
import jax.numpy as jnp
from jax import lax
from jax.sharding import PartitionSpec as P

LAPLACE_COEFS = (-205.0 / 72.0, 8.0 / 5.0, -1.0 / 5.0, 8.0 / 315.0, -1.0 / 560.0)


def padded_2(block, sides, width):
    for axis, dim in sides:
        count = lax.axis_size(axis)
        forward = [(i, i + 1) for i in range(count - 1)]
        backward = [(target, source) for source, target in forward]
        low = lax.ppermute(
            lax.slice_in_dim(block, block.shape[dim] - width, None, axis=dim), axis, forward
        )
        high = lax.ppermute(lax.slice_in_dim(block, 0, width, axis=dim), axis, backward)
        block = jnp.concatenate([low, block, high], axis=dim)
    return block


def laplace_padded(padded_xy, size_x, size_y, size_z):
    padded = jnp.pad(padded_xy, ((0, 0), (0, 0), (4, 4)))
    center = padded[4 : 4 + size_x, 4 : 4 + size_y, 4 : 4 + size_z]
    total = 3.0 * LAPLACE_COEFS[0] * center
    for offset in range(1, 5):
        weight = LAPLACE_COEFS[offset]
        total = total + weight * (
            padded[4 + offset : 4 + offset + size_x, 4 : 4 + size_y, 4 : 4 + size_z]
            + padded[4 - offset : 4 - offset + size_x, 4 : 4 + size_y, 4 : 4 + size_z]
        )
        total = total + weight * (
            padded[4 : 4 + size_x, 4 + offset : 4 + offset + size_y, 4 : 4 + size_z]
            + padded[4 : 4 + size_x, 4 - offset : 4 - offset + size_y, 4 : 4 + size_z]
        )
        total = total + weight * (
            padded[4 : 4 + size_x, 4 : 4 + size_y, 4 + offset : 4 + offset + size_z]
            + padded[4 : 4 + size_x, 4 : 4 + size_y, 4 - offset : 4 - offset + size_z]
        )
    return total


def extend(field):
    return padded_2(field, (("gx", 0), ("gy", 1)), 4)


def restrict(fine):
    size_x, size_y, size_z = fine.shape
    return fine.reshape(size_x // 2, 2, size_y // 2, 2, size_z // 2, 2).mean(axis=(1, 3, 5))


def local(adj_prev, adj_cur, fwd_accel, courant2, traces, weights, rblock, column, counts):
    previous = adj_prev[0]
    current = adj_cur[0]
    size_x, size_y, size_z = current.shape
    steps = fwd_accel.shape[1]
    slots = weights.shape[2]
    recv_block = weights.shape[3]
    gathered = lax.all_gather(traces, ("gx", "gy"), axis=2, tiled=True)
    blocks = gathered[0].reshape(steps, -1, recv_block)
    picked = jnp.take(blocks, rblock[0, 0], axis=1)
    contrib = jnp.einsum("tsr,srz->tsz", picked, weights[0, 0], preferred_element_type=jnp.float32)
    live_slots = (jnp.arange(slots, dtype=jnp.int32) < counts[0, 0]).astype(jnp.float32)
    onehot = (
        column[0, 0][:, None] == jnp.arange(size_x * size_y, dtype=jnp.int32)[None, :]
    ).astype(jnp.float32) * live_slots[:, None]
    source = jnp.einsum("sc,tsz->tcz", onehot, contrib, precision=lax.Precision.HIGHEST).reshape(
        steps, size_x, size_y, size_z
    )
    fine = jnp.zeros(current.shape, jnp.float32)
    for step_index in range(steps):
        padded_xy = extend(current)
        next_field = (
            2.0 * current
            - previous
            + courant2 * laplace_padded(padded_xy, size_x, size_y, size_z)
            + source[step_index]
        )
        fine = fine + fwd_accel[0, step_index].astype(jnp.float32) * next_field
        previous, current = (current, next_field)
    gradient = lax.psum(restrict(fine), "shot")
    return (previous[None], current[None], gradient)


def solution(mesh):
    return jax.shard_map(
        local,
        mesh=mesh,
        in_specs=(
            P("shot", "gx", "gy", None),
            P("shot", "gx", "gy", None),
            P("shot", None, "gx", "gy", None),
            P("gx", "gy", None),
            P("shot", None, ("gx", "gy")),
            P("gx", "gy", None, None, None),
            P("gx", "gy", None),
            P("gx", "gy", None),
            P("gx", "gy"),
        ),
        out_specs=(P("shot", "gx", "gy", None), P("shot", "gx", "gy", None), P("gx", "gy", None)),
        check_vma=False,
    )
```

profile of v0, /device:TPU:0, one launch (start us, length us, event | category | flops | bytes accessed | tf_op | source)
XLA Modules:
  0.0 203.9 jit_solution(15450160707005926613)
XLA Ops:
  8.2 1.3 collective-permute-start
  9.5 4.9 %collective-permute-start.1 = (f32[4,16,256]{2,1,0:T(8,128)S(1)}, f32[4,16,256]{2,1,0:T(8,128)S(1)}, u32[]{:S(2)}, u32[]{:S(2)}) collective-permute-start(f32[4,16,256]{2,1,0:T(8,128)S(1)} %get-tuple-element.32), channel_id=1, source_target_pairs={{0,16},{1,17},{2,18},{3,19},{4,20},{5,21},{6,22},{7,23},{8,24},{9,... | collective-permute-start | bytes 196616 | tf_op jit(solution)/shard_map/ppermute | solution.py:14
  17.2 10.4 %all_gather.3 = bf16[1,4,512]{1,0,2:T(2,128)(2,1)S(1)} all-gather(bf16[1,4,64]{1,0,2:T(2,128)(2,1)S(1)} %copy.21), channel_id=1, replica_groups=mesh['gx'=2,'gy'=4,'shot'=4] {'gx','gy'}, dimensions={2}, use_global_device_ids=true | all-gather | bytes 4608 | tf_op jit(solution)/shard_map/all_gather | solution.py:59
  28.8 1.9 convolution_bitcast_fusion
  30.8 2.3 %collective-permute-start.3 = (f32[40,4,256]{2,1,0:T(4,128)S(1)}, f32[40,4,256]{2,1,0:T(4,128)S(1)}, u32[]{:S(2)}, u32[]{:S(2)}) collective-permute-start(f32[40,4,256]{2,1,0:T(4,128)S(1)} %get-tuple-element.23), channel_id=1, source_target_pairs={{0,4},{4,8},{8,12},{1,5},{5,9},{9,13},{2,6},{6,10},{10,14},{3,7},{... | collective-permute-start | bytes 491528 | tf_op jit(solution)/shard_map/ppermute | solution.py:14
  33.0 1.3 collective-permute-start.2
  38.3 2.0 fusion.93
  40.3 1.4 collective-permute-start.4
  41.8 4.5 %collective-permute-start.5 = (f32[4,16,256]{2,1,0:T(8,128)S(1)}, f32[4,16,256]{2,1,0:T(8,128)S(1)}, u32[]{:S(2)}, u32[]{:S(2)}) collective-permute-start(f32[4,16,256]{2,1,0:T(8,128)S(1)} %get-tuple-element.30), channel_id=1, source_target_pairs={{0,16},{1,17},{2,18},{3,19},{4,20},{5,21},{6,22},{7,23},{8,24},{9,... | collective-permute-start | bytes 196616 | tf_op jit(solution)/shard_map/ppermute | solution.py:14
  46.6 1.6 collective-permute-done.5
  49.0 4.1 %collective-permute-start.7 = (f32[40,4,256]{2,1,0:T(4,128)}, f32[40,4,256]{2,1,0:T(4,128)S(1)}, u32[]{:S(2)}, u32[]{:S(2)}) collective-permute-start(f32[40,4,256]{2,1,0:T(4,128)} %get-tuple-element.19), channel_id=1, source_target_pairs={{0,4},{4,8},{8,12},{1,5},{5,9},{9,13},{2,6},{6,10},{10,14},{3,7},{... | collective-permute-start | bytes 491528 | tf_op jit(solution)/shard_map/ppermute | solution.py:14
  54.7 2.6 %collective-permute-done.6 = f32[40,4,256]{2,1,0:T(4,128)} collective-permute-done((f32[40,4,256]{2,1,0:T(4,128)}, f32[40,4,256]{2,1,0:T(4,128)}, u32[]{:S(2)}, u32[]{:S(2)}) %collective-permute-start.6) | collective-permute-done | bytes 163872 | tf_op jit(solution)/shard_map/ppermute | solution.py:17
  57.2 1.7 select_maximum_fusion.8
  60.0 2.0 fusion.66
  62.1 1.4 collective-permute-start.8
  63.5 4.5 %collective-permute-start.9 = (f32[4,16,256]{2,1,0:T(8,128)S(1)}, f32[4,16,256]{2,1,0:T(8,128)S(1)}, u32[]{:S(2)}, u32[]{:S(2)}) collective-permute-start(f32[4,16,256]{2,1,0:T(8,128)S(1)} %get-tuple-element.28), channel_id=1, source_target_pairs={{0,16},{1,17},{2,18},{3,19},{4,20},{5,21},{6,22},{7,23},{8,24},{9,... | collective-permute-start | bytes 196616 | tf_op jit(solution)/shard_map/ppermute | solution.py:14
  68.3 1.6 collective-permute-done.9
  70.7 4.6 %collective-permute-start.11 = (f32[40,4,256]{2,1,0:T(4,128)}, f32[40,4,256]{2,1,0:T(4,128)S(1)}, u32[]{:S(2)}, u32[]{:S(2)}) collective-permute-start(f32[40,4,256]{2,1,0:T(4,128)} %get-tuple-element.15), channel_id=1, source_target_pairs={{0,4},{4,8},{8,12},{1,5},{5,9},{9,13},{2,6},{6,10},{10,14},{3,7},{... | collective-permute-start | bytes 491528 | tf_op jit(solution)/shard_map/ppermute | solution.py:14
  76.8 2.6 %collective-permute-done.10 = f32[40,4,256]{2,1,0:T(4,128)} collective-permute-done((f32[40,4,256]{2,1,0:T(4,128)}, f32[40,4,256]{2,1,0:T(4,128)}, u32[]{:S(2)}, u32[]{:S(2)}) %collective-permute-start.10) | collective-permute-done | bytes 163872 | tf_op jit(solution)/shard_map/ppermute | solution.py:17
  79.4 1.7 select_maximum_fusion.4
  82.2 2.0 fusion.39
  84.2 4.4 %collective-permute-start.13 = (f32[4,16,256]{2,1,0:T(8,128)S(1)}, f32[4,16,256]{2,1,0:T(8,128)S(1)}, u32[]{:S(2)}, u32[]{:S(2)}) collective-permute-start(f32[4,16,256]{2,1,0:T(8,128)S(1)} %get-tuple-element.25), channel_id=1, source_target_pairs={{0,16},{1,17},{2,18},{3,19},{4,20},{5,21},{6,22},{7,23},{8,24},{9,... | collective-permute-start | bytes 196616 | tf_op jit(solution)/shard_map/ppermute | solution.py:14
  90.5 4.3 %collective-permute-done.12 = f32[4,16,256]{2,1,0:T(8,128)S(1)} collective-permute-done((f32[4,16,256]{2,1,0:T(8,128)S(1)}, f32[4,16,256]{2,1,0:T(8,128)S(1)}, u32[]{:S(2)}, u32[]{:S(2)}) %collective-permute-start.12) | collective-permute-done | bytes 65568 | tf_op jit(solution)/shard_map/ppermute | solution.py:17
  95.6 4.3 %collective-permute-start.15 = (f32[40,4,256]{2,1,0:T(4,128)}, f32[40,4,256]{2,1,0:T(4,128)S(1)}, u32[]{:S(2)}, u32[]{:S(2)}) collective-permute-start(f32[40,4,256]{2,1,0:T(4,128)} %get-tuple-element.11), channel_id=1, source_target_pairs={{0,4},{4,8},{8,12},{1,5},{5,9},{9,13},{2,6},{6,10},{10,14},{3,7},{... | collective-permute-start | bytes 491528 | tf_op jit(solution)/shard_map/ppermute | solution.py:14
  99.9 1.5 collective-permute-start.14
  102.4 1.9 collective-permute-done.14
  104.3 1.7 select_maximum_fusion
  107.4 2.9 %fusion.149 = (f32[32,16,256]{2,1,0:T(8,128)S(1)}, f32[32,16,256]{2,1,0:T(8,128)}) fusion(f32[32,16,256]{2,1,0:T(8,128)S(1)} %fusion.39, f32[32,16,256]{2,1,0:T(8,128)S(1)} %fusion.66, f32[32,16,256]{2,1,0:T(8,128)S(1)} %fusion.93, bf16[1,4,32,16,256]{4,3,2,1,0:T(8,128)(2,1)S(1)} %copy-done.8, f32[32,16,256]{2,1,0:T(8,128)S(1)} %bitcast.55, ...), kind=kLoop, calls=%fused_computation.267 | loop fusion | flops 7995392 | bytes 13238272 | tf_op jit(solution)/shard_map/add | solution.py:79
  110.3 34.8 %reshape.68 = f32[16,2,8,2,128,2]{5,4,3,2,1,0:T(8,128)} reshape(f32[32,16,256]{2,1,0:T(8,128)S(1)} %get-tuple-element.3) | data formatting | bytes 1048576 | tf_op jit(solution)/shard_map/reshape | solution.py:49
  145.1 12.2 %reduce_sum.9 = f32[16,8,128]{2,1,0:T(8,128)S(1)} reduce(f32[16,2,8,2,128,2]{5,4,3,2,1,0:T(8,128)} %reshape.68, f32[]{:T(128)} %constant.9.clone.1), dimensions={1,3,5}, to_apply=%region_0.1 | reduce | flops 114688 | bytes 589828 | tf_op jit(solution)/shard_map/reduce_sum | solution.py:49
  158.0 37.6 %all-reduce.6.cloned.1.call-done = f32[16,8,128]{2,1,0:T(8,128)} async-done(((f32[16,8,128]{2,1,0:T(8,128)}), f32[16,8,128]{2,1,0:T(8,128)}) %all-reduce.6.cloned.1.call-update) | async-done | bytes 65552 | tf_op jit(solution)/shard_map/psum | solution.py:81
  195.6 1.5 copy.33
  (66 shorter events, 21.3 us)
Async XLA Ops:
  7.2 21.3 %copy-start = (bf16[1,1,64,16,256]{4,3,2,1,0:T(8,128)(2,1)S(1)}, bf16[1,1,64,16,256]{4,3,2,1,0:T(8,128)(2,1)}, u32[]{:S(2)}) copy-start(bf16[1,1,64,16,256]{4,3,2,1,0:T(8,128)(2,1)} %param.14) | copy-start | bytes 1572868
  7.2 21.6 %copy-start.10 = (s32[1,1,64]{2,1,0:T(1,128)S(1)}, s32[1,1,64]{2,1,0:T(1,128)}, u32[]{:S(2)}) copy-start(s32[1,1,64]{2,1,0:T(1,128)} %param.16) | copy-start | bytes 772
  7.2 188.4 %all-reduce.6.cloned.1.call-start = ((), (), s32[]{:S(2)}) async-start(), calls=%async_computation | async-start | bytes 131072 | tf_op jit(solution)/shard_map/psum | solution.py:81
  8.2 22.5 %collective-permute-start = (f32[4,16,256]{2,1,0:T(8,128)S(1)}, f32[4,16,256]{2,1,0:T(8,128)S(1)}, u32[]{:S(2)}, u32[]{:S(2)}) collective-permute-start(f32[4,16,256]{2,1,0:T(8,128)S(1)} %get-tuple-element.31), channel_id=1, source_target_pairs={{16,0},{17,1},{18,2},{19,3},{20,4},{21,5},{22,6},{23,7},{24,8},{25... | collective-permute-start | bytes 196616 | tf_op jit(solution)/shard_map/ppermute | solution.py:17
  9.5 21.2 %collective-permute-start.1 = (f32[4,16,256]{2,1,0:T(8,128)S(1)}, f32[4,16,256]{2,1,0:T(8,128)S(1)}, u32[]{:S(2)}, u32[]{:S(2)}) collective-permute-start(f32[4,16,256]{2,1,0:T(8,128)S(1)} %get-tuple-element.32), channel_id=1, source_target_pairs={{0,16},{1,17},{2,18},{3,19},{4,20},{5,21},{6,22},{7,23},{8,24},{9,... | collective-permute-start | bytes 196616 | tf_op jit(solution)/shard_map/ppermute | solution.py:14
  28.5 2.2 %copy-start.1 = (f32[1,32,16,256]{3,2,1,0:T(8,128)S(1)}, f32[1,32,16,256]{3,2,1,0:T(8,128)}, u32[]{:S(2)}) copy-start(f32[1,32,16,256]{3,2,1,0:T(8,128)} %param.10) | copy-start | bytes 1572868
  30.8 5.0 %collective-permute-start.3 = (f32[40,4,256]{2,1,0:T(4,128)S(1)}, f32[40,4,256]{2,1,0:T(4,128)S(1)}, u32[]{:S(2)}, u32[]{:S(2)}) collective-permute-start(f32[40,4,256]{2,1,0:T(4,128)S(1)} %get-tuple-element.23), channel_id=1, source_target_pairs={{0,4},{4,8},{8,12},{1,5},{5,9},{9,13},{2,6},{6,10},{10,14},{3,7},{... | collective-permute-start | bytes 491528 | tf_op jit(solution)/shard_map/ppermute | solution.py:14
  33.0 3.3 %collective-permute-start.2 = (f32[40,4,256]{2,1,0:T(4,128)S(1)}, f32[40,4,256]{2,1,0:T(4,128)S(1)}, u32[]{:S(2)}, u32[]{:S(2)}) collective-permute-start(f32[40,4,256]{2,1,0:T(4,128)S(1)} %get-tuple-element.24), channel_id=1, source_target_pairs={{4,0},{8,4},{12,8},{5,1},{9,5},{13,9},{6,2},{10,6},{14,10},{7,3},{... | collective-permute-start | bytes 491528 | tf_op jit(solution)/shard_map/ppermute | solution.py:17
  37.1 1.0 copy-start.3
  37.1 1.2 copy-start.9
  40.3 14.1 %copy-start.7 = (f32[1,512,256]{1,2,0:T(8,128)S(1)}, f32[1,512,256]{1,2,0:T(8,128)}, u32[]{:S(2)}) copy-start(f32[1,512,256]{1,2,0:T(8,128)} %get-tuple-element.7) | copy-start | bytes 1572868
  40.3 6.3 %collective-permute-start.4 = (f32[4,16,256]{2,1,0:T(8,128)S(1)}, f32[4,16,256]{2,1,0:T(8,128)S(1)}, u32[]{:S(2)}, u32[]{:S(2)}) collective-permute-start(f32[4,16,256]{2,1,0:T(8,128)S(1)} %get-tuple-element.29), channel_id=1, source_target_pairs={{16,0},{17,1},{18,2},{19,3},{20,4},{21,5},{22,6},{23,7},{24,8},{25... | collective-permute-start | bytes 196616 | tf_op jit(solution)/shard_map/ppermute | solution.py:17
  41.8 6.4 %collective-permute-start.5 = (f32[4,16,256]{2,1,0:T(8,128)S(1)}, f32[4,16,256]{2,1,0:T(8,128)S(1)}, u32[]{:S(2)}, u32[]{:S(2)}) collective-permute-start(f32[4,16,256]{2,1,0:T(8,128)S(1)} %get-tuple-element.30), channel_id=1, source_target_pairs={{0,16},{1,17},{2,18},{3,19},{4,20},{5,21},{6,22},{7,23},{8,24},{9,... | collective-permute-start | bytes 196616 | tf_op jit(solution)/shard_map/ppermute | solution.py:14
  49.0 5.6 %collective-permute-start.7 = (f32[40,4,256]{2,1,0:T(4,128)}, f32[40,4,256]{2,1,0:T(4,128)S(1)}, u32[]{:S(2)}, u32[]{:S(2)}) collective-permute-start(f32[40,4,256]{2,1,0:T(4,128)} %get-tuple-element.19), channel_id=1, source_target_pairs={{0,4},{4,8},{8,12},{1,5},{5,9},{9,13},{2,6},{6,10},{10,14},{3,7},{... | collective-permute-start | bytes 491528 | tf_op jit(solution)/shard_map/ppermute | solution.py:14
  53.1 4.1 %collective-permute-start.6 = (f32[40,4,256]{2,1,0:T(4,128)}, f32[40,4,256]{2,1,0:T(4,128)}, u32[]{:S(2)}, u32[]{:S(2)}) collective-permute-start(f32[40,4,256]{2,1,0:T(4,128)} %get-tuple-element.20), channel_id=1, source_target_pairs={{4,0},{8,4},{12,8},{5,1},{9,5},{13,9},{6,2},{10,6},{14,10},{7,3},{... | collective-permute-start | bytes 491528 | tf_op jit(solution)/shard_map/ppermute | solution.py:17
  62.0 14.6 %copy-start.6 = (f32[1,512,256]{1,2,0:T(8,128)S(1)}, f32[1,512,256]{1,2,0:T(8,128)}, u32[]{:S(2)}) copy-start(f32[1,512,256]{1,2,0:T(8,128)} %get-tuple-element.6) | copy-start | bytes 1572868
  62.1 6.3 %collective-permute-start.8 = (f32[4,16,256]{2,1,0:T(8,128)S(1)}, f32[4,16,256]{2,1,0:T(8,128)S(1)}, u32[]{:S(2)}, u32[]{:S(2)}) collective-permute-start(f32[4,16,256]{2,1,0:T(8,128)S(1)} %get-tuple-element.27), channel_id=1, source_target_pairs={{16,0},{17,1},{18,2},{19,3},{20,4},{21,5},{22,6},{23,7},{24,8},{25... | collective-permute-start | bytes 196616 | tf_op jit(solution)/shard_map/ppermute | solution.py:17
  63.5 6.4 %collective-permute-start.9 = (f32[4,16,256]{2,1,0:T(8,128)S(1)}, f32[4,16,256]{2,1,0:T(8,128)S(1)}, u32[]{:S(2)}, u32[]{:S(2)}) collective-permute-start(f32[4,16,256]{2,1,0:T(8,128)S(1)} %get-tuple-element.28), channel_id=1, source_target_pairs={{0,16},{1,17},{2,18},{3,19},{4,20},{5,21},{6,22},{7,23},{8,24},{9,... | collective-permute-start | bytes 196616 | tf_op jit(solution)/shard_map/ppermute | solution.py:14
  70.7 6.1 %collective-permute-start.11 = (f32[40,4,256]{2,1,0:T(4,128)}, f32[40,4,256]{2,1,0:T(4,128)S(1)}, u32[]{:S(2)}, u32[]{:S(2)}) collective-permute-start(f32[40,4,256]{2,1,0:T(4,128)} %get-tuple-element.15), channel_id=1, source_target_pairs={{0,4},{4,8},{8,12},{1,5},{5,9},{9,13},{2,6},{6,10},{10,14},{3,7},{... | collective-permute-start | bytes 491528 | tf_op jit(solution)/shard_map/ppermute | solution.py:14
  75.3 4.1 %collective-permute-start.10 = (f32[40,4,256]{2,1,0:T(4,128)}, f32[40,4,256]{2,1,0:T(4,128)}, u32[]{:S(2)}, u32[]{:S(2)}) collective-permute-start(f32[40,4,256]{2,1,0:T(4,128)} %get-tuple-element.16), channel_id=1, source_target_pairs={{4,0},{8,4},{12,8},{5,1},{9,5},{13,9},{6,2},{10,6},{14,10},{7,3},{... | collective-permute-start | bytes 491528 | tf_op jit(solution)/shard_map/ppermute | solution.py:17
  84.2 23.0 %copy-start.2 = (f32[32,16,256]{2,1,0:T(8,128)}, f32[32,16,256]{2,1,0:T(8,128)S(1)}, u32[]{:S(2)}) copy-start(f32[32,16,256]{2,1,0:T(8,128)S(1)} %fusion.39) | copy-start | bytes 1572868
  84.2 17.2 %copy-start.5 = (f32[1,512,256]{1,2,0:T(8,128)S(1)}, f32[1,512,256]{1,2,0:T(8,128)}, u32[]{:S(2)}) copy-start(f32[1,512,256]{1,2,0:T(8,128)} %get-tuple-element.5) | copy-start | bytes 1572868
  84.2 6.3 %collective-permute-start.13 = (f32[4,16,256]{2,1,0:T(8,128)S(1)}, f32[4,16,256]{2,1,0:T(8,128)S(1)}, u32[]{:S(2)}, u32[]{:S(2)}) collective-permute-start(f32[4,16,256]{2,1,0:T(8,128)S(1)} %get-tuple-element.25), channel_id=1, source_target_pairs={{0,16},{1,17},{2,18},{3,19},{4,20},{5,21},{6,22},{7,23},{8,24},{9,... | collective-permute-start | bytes 196616 | tf_op jit(solution)/shard_map/ppermute | solution.py:14
  88.6 6.2 %collective-permute-start.12 = (f32[4,16,256]{2,1,0:T(8,128)S(1)}, f32[4,16,256]{2,1,0:T(8,128)S(1)}, u32[]{:S(2)}, u32[]{:S(2)}) collective-permute-start(f32[4,16,256]{2,1,0:T(8,128)S(1)} %get-tuple-element.26), channel_id=1, source_target_pairs={{16,0},{17,1},{18,2},{19,3},{20,4},{21,5},{22,6},{23,7},{24,8},{25... | collective-permute-start | bytes 196616 | tf_op jit(solution)/shard_map/ppermute | solution.py:17
  95.6 6.8 %collective-permute-start.15 = (f32[40,4,256]{2,1,0:T(4,128)}, f32[40,4,256]{2,1,0:T(4,128)S(1)}, u32[]{:S(2)}, u32[]{:S(2)}) collective-permute-start(f32[40,4,256]{2,1,0:T(4,128)} %get-tuple-element.11), channel_id=1, source_target_pairs={{0,4},{4,8},{8,12},{1,5},{5,9},{9,13},{2,6},{6,10},{10,14},{3,7},{... | collective-permute-start | bytes 491528 | tf_op jit(solution)/shard_map/ppermute | solution.py:14
  99.9 4.4 %collective-permute-start.14 = (f32[40,4,256]{2,1,0:T(4,128)}, f32[40,4,256]{2,1,0:T(4,128)}, u32[]{:S(2)}, u32[]{:S(2)}) collective-permute-start(f32[40,4,256]{2,1,0:T(4,128)} %get-tuple-element.12), channel_id=1, source_target_pairs={{4,0},{8,4},{12,8},{5,1},{9,5},{13,9},{6,2},{10,6},{14,10},{7,3},{... | collective-permute-start | bytes 491528 | tf_op jit(solution)/shard_map/ppermute | solution.py:17
  106.0 1.2 copy-start.4
  106.0 1.5 copy-start.8
Sparse Core Ops, SparseCore 0:
  158.1 37.4 all-reduce.5
where the time goes:
time: 205 us; the launch traced here: 204 us
  waiting for transfers between devices  53.9 us (26%)
  starting transfers between devices  44.5 us (22%)
  local copies, waits for them, and re-layouts  43 us (21%)
  other arithmetic  34.7 us (17%)
  between operations  15.2 us (7%)
  blocking collectives  10.4 us (5%)
  matrix products  2.15 us (1%)
    psum x1, waiting for transfers between devices, local(): gradient = lax.psum(restrict(fine), 'shot')  37.6 us
    reshape x1, local copies, waits for them, and re-layouts, restrict(): fine.reshape(size_x // 2, 2, size_y // 2, 2, size_z // 2, 2)  34.8 us
    ppermute x8, starting transfers between devices, padded_2(): lax.ppermute(lax.slice_in_dim(block, block.shape[dim] - width, None, axis...  33.7 us
    ppermute x8, waiting for transfers between devices, padded_2(): lax.ppermute(lax.slice_in_dim(block, 0, width, axis=dim), axis, backward)  12.5 us
    reduce_sum x1, other arithmetic, restrict(): fine.reshape(size_x // 2, 2, size_y // 2, 2, size_z // 2, 2)  12.2 us
    concatenate x12, other arithmetic, padded_2(): block = jnp.concatenate([low, block, high], axis=dim)  11.7 us
    ppermute x8, starting transfers between devices, padded_2(): lax.ppermute(lax.slice_in_dim(block, 0, width, axis=dim), axis, backward)  10.8 us
    all_gather x1, blocking collectives, local(): gathered = lax.all_gather(traces, ('gx', 'gy'), axis=2, tiled=True)  10.4 us
  transfers between devices with their start and end apart: 17, of which 11 were waited for; matrix products, arithmetic and copies ran while one was open for 4% of the time, Pallas kernels for 0%

commit v1 on v0

--- a/solution.py
+++ b/solution.py
@@ -78,7 +78,7 @@
         )
         fine = fine + fwd_accel[0, step_index].astype(jnp.float32) * next_field
         previous, current = (current, next_field)
-    gradient = lax.psum(restrict(fine), "shot")
+    gradient = jnp.sum(lax.all_gather(restrict(fine), "shot"), axis=0)
     return (previous[None], current[None], gradient)
 
 

time: 205 us -> 168 us (0.82)
  waiting for transfers between devices: 53.9 us -> 16.3 us
  blocking collectives: 10.4 us -> 25.2 us
  between operations: 15.2 us -> 1.8 us
    psum x1 -> x0, waiting for transfers between devices: 37.6 us -> none  [local(): gradient = lax.psum(restrict(fine), 'shot')]
    all_gather x0 -> x1, blocking collectives: none -> 14.8 us  [local(): gradient = jnp.sum(lax.all_gather(restrict(fine), 'shot'), axis=0)]
  transfers between devices with their start and end apart: 17 -> 16, of which waited for: 11 -> 10; matrix products, arithmetic and copies ran while one was open for 4% -> 5% of each run, Pallas kernels for 0% -> 0%
where the time goes in v1:
time: 168 us; the launch traced here: 166 us
  starting transfers between devices  44.4 us (26%)
  local copies, waits for them, and re-layouts  41.6 us (25%)
  other arithmetic  34.8 us (21%)
  blocking collectives  25.2 us (15%)
  waiting for transfers between devices  16.3 us (10%)
  matrix products  2.15 us (1%)
  between operations  1.8 us (1%)
    reshape x1, local copies, waits for them, and re-layouts, restrict(): fine.reshape(size_x // 2, 2, size_y // 2, 2, size_z // 2, 2)  34.8 us
    ppermute x8, starting transfers between devices, padded_2(): lax.ppermute(lax.slice_in_dim(block, block.shape[dim] - width, None, axis...  33.7 us
    all_gather x1, blocking collectives, local(): gradient = jnp.sum(lax.all_gather(restrict(fine), 'shot'), axis=0)  14.8 us
    ppermute x8, waiting for transfers between devices, padded_2(): lax.ppermute(lax.slice_in_dim(block, 0, width, axis=dim), axis, backward)  12.6 us
    reduce_sum x1, other arithmetic, restrict(): fine.reshape(size_x // 2, 2, size_y // 2, 2, size_z // 2, 2)  12.2 us
    concatenate x12, other arithmetic, padded_2(): block = jnp.concatenate([low, block, high], axis=dim)  11.7 us
    ppermute x8, starting transfers between devices, padded_2(): lax.ppermute(lax.slice_in_dim(block, 0, width, axis=dim), axis, backward)  10.8 us
    all_gather x1, blocking collectives, local(): gathered = lax.all_gather(traces, ('gx', 'gy'), axis=2, tiled=True)  10.4 us
  transfers between devices with their start and end apart: 16, of which 10 were waited for; matrix products, arithmetic and copies ran while one was open for 5% of the time, Pallas kernels for 0%

profile of v1, /device:TPU:0, one launch (start us, length us, event | category | flops | bytes accessed | tf_op | source)
XLA Modules:
  0.0 166.3 jit_solution(9032730978474133348)
XLA Ops:
  1.6 1.3 collective-permute-start
  2.9 4.9 %collective-permute-start.1 = (f32[4,16,256]{2,1,0:T(8,128)S(1)}, f32[4,16,256]{2,1,0:T(8,128)S(1)}, u32[]{:S(2)}, u32[]{:S(2)}) collective-permute-start(f32[4,16,256]{2,1,0:T(8,128)S(1)} %get-tuple-element.32), channel_id=1, source_target_pairs={{0,16},{1,17},{2,18},{3,19},{4,20},{5,21},{6,22},{7,23},{8,24},{9,... | collective-permute-start | bytes 196616 | tf_op jit(solution)/shard_map/ppermute | solution.py:14
  10.6 10.4 %all_gather.7 = bf16[1,4,512]{1,0,2:T(2,128)(2,1)S(1)} all-gather(bf16[1,4,64]{1,0,2:T(2,128)(2,1)S(1)} %copy.21), channel_id=1, replica_groups=mesh['gx'=2,'gy'=4,'shot'=4] {'gx','gy'}, dimensions={2}, use_global_device_ids=true | all-gather | bytes 4608 | tf_op jit(solution)/shard_map/all_gather | solution.py:59
  22.2 1.9 %convolution_bitcast_fusion = f32[4,512,256]{1,2,0:T(8,128)S(1)} fusion(f32[4,64,256]{2,0,1:T(4,128)S(1)} %convolution_bitcast_fusion.1, f32[64]{0:T(128)S(1)} %compare_convert_fusion, s32[64]{0:T(128)S(1)} %bitcast.62), kind=kOutput, calls=%fused_computation.3 | convolution fusion | flops 402718720 | bytes 2359808 | tf_op jit(solution)/shard_map/sc,tsz->tcz/dot_general | solution.py:67
  24.2 2.3 %collective-permute-start.3 = (f32[40,4,256]{2,1,0:T(4,128)S(1)}, f32[40,4,256]{2,1,0:T(4,128)S(1)}, u32[]{:S(2)}, u32[]{:S(2)}) collective-permute-start(f32[40,4,256]{2,1,0:T(4,128)S(1)} %get-tuple-element.23), channel_id=1, source_target_pairs={{0,4},{4,8},{8,12},{1,5},{5,9},{9,13},{2,6},{6,10},{10,14},{3,7},{... | collective-permute-start | bytes 491528 | tf_op jit(solution)/shard_map/ppermute | solution.py:14
  26.5 1.3 collective-permute-start.2
  31.7 2.0 %fusion.93 = f32[32,16,256]{2,1,0:T(8,128)S(1)} fusion(f32[32,16,256]{2,1,0:T(8,128)S(1)} %bitcast.57, f32[32,16,256]{2,1,0:T(8,128)S(1)} %copy-done.3, f32[32,16,256]{2,1,0:T(8,128)S(1)} %bitcast.54, f32[4,16,256]{2,1,0:T(8,128)S(1)} %collective-permute-done.1, f32[4,16,256]{2,1,0:T(8,128)S(1)} %collective-permute-done, ...), kind=kLoop, calls=%fused_computation.170 | loop fusion | flops 6553600 | bytes 11141120 | tf_op jit(solution)/shard_map/add | solution.py:74
  33.8 1.4 collective-permute-start.4
  35.2 4.5 %collective-permute-start.5 = (f32[4,16,256]{2,1,0:T(8,128)S(1)}, f32[4,16,256]{2,1,0:T(8,128)S(1)}, u32[]{:S(2)}, u32[]{:S(2)}) collective-permute-start(f32[4,16,256]{2,1,0:T(8,128)S(1)} %get-tuple-element.30), channel_id=1, source_target_pairs={{0,16},{1,17},{2,18},{3,19},{4,20},{5,21},{6,22},{7,23},{8,24},{9,... | collective-permute-start | bytes 196616 | tf_op jit(solution)/shard_map/ppermute | solution.py:14
  40.1 1.6 collective-permute-done.5
  42.4 4.1 %collective-permute-start.7 = (f32[40,4,256]{2,1,0:T(4,128)}, f32[40,4,256]{2,1,0:T(4,128)S(1)}, u32[]{:S(2)}, u32[]{:S(2)}) collective-permute-start(f32[40,4,256]{2,1,0:T(4,128)} %get-tuple-element.19), channel_id=1, source_target_pairs={{0,4},{4,8},{8,12},{1,5},{5,9},{9,13},{2,6},{6,10},{10,14},{3,7},{... | collective-permute-start | bytes 491528 | tf_op jit(solution)/shard_map/ppermute | solution.py:14
  46.5 1.3 collective-permute-start.6
  48.1 2.6 %collective-permute-done.6 = f32[40,4,256]{2,1,0:T(4,128)} collective-permute-done((f32[40,4,256]{2,1,0:T(4,128)}, f32[40,4,256]{2,1,0:T(4,128)}, u32[]{:S(2)}, u32[]{:S(2)}) %collective-permute-start.6) | collective-permute-done | bytes 163872 | tf_op jit(solution)/shard_map/ppermute | solution.py:17
  50.6 1.7 %select_maximum_fusion.8 = f32[40,24,264]{2,1,0:T(8,128)S(1)} fusion(f32[40,4,256]{2,1,0:T(4,128)} %collective-permute-done.6, f32[40,4,256]{2,1,0:T(4,128)S(1)} %collective-permute-done.7, f32[4,16,256]{2,1,0:T(8,128)S(1)} %collective-permute-done.4, f32[32,16,256]{2,1,0:T(8,128)S(1)} %fusion.93, f32[4,16,256]{2,1,0:T(8,128)S(1)} %collective-permute-done.5), kind=kLoop, calls=%fused_computation.12 | loop fusion | flops 3041280 | bytes 1996800 | tf_op jit(solution)/shard_map/concatenate | solution.py:18
  53.4 2.0 %fusion.66 = f32[32,16,256]{2,1,0:T(8,128)S(1)} fusion(f32[32,16,256]{2,1,0:T(8,128)S(1)} %bitcast.58, f32[32,16,256]{2,1,0:T(8,128)S(1)} %copy-done.3, f32[32,16,256]{2,1,0:T(8,128)S(1)} %fusion.93, f32[4,16,256]{2,1,0:T(8,128)S(1)} %collective-permute-done.5, f32[4,16,256]{2,1,0:T(8,128)S(1)} %collective-permute-done.4, ...), kind=kLoop, calls=%fused_computation.143 | loop fusion | flops 6553600 | bytes 11141120 | tf_op jit(solution)/shard_map/add | solution.py:74
  55.5 1.4 collective-permute-start.8
  56.9 4.5 %collective-permute-start.9 = (f32[4,16,256]{2,1,0:T(8,128)S(1)}, f32[4,16,256]{2,1,0:T(8,128)S(1)}, u32[]{:S(2)}, u32[]{:S(2)}) collective-permute-start(f32[4,16,256]{2,1,0:T(8,128)S(1)} %get-tuple-element.28), channel_id=1, source_target_pairs={{0,16},{1,17},{2,18},{3,19},{4,20},{5,21},{6,22},{7,23},{8,24},{9,... | collective-permute-start | bytes 196616 | tf_op jit(solution)/shard_map/ppermute | solution.py:14
  61.8 1.6 collective-permute-done.9
  64.1 4.6 %collective-permute-start.11 = (f32[40,4,256]{2,1,0:T(4,128)}, f32[40,4,256]{2,1,0:T(4,128)S(1)}, u32[]{:S(2)}, u32[]{:S(2)}) collective-permute-start(f32[40,4,256]{2,1,0:T(4,128)} %get-tuple-element.15), channel_id=1, source_target_pairs={{0,4},{4,8},{8,12},{1,5},{5,9},{9,13},{2,6},{6,10},{10,14},{3,7},{... | collective-permute-start | bytes 491528 | tf_op jit(solution)/shard_map/ppermute | solution.py:14
  70.2 2.6 %collective-permute-done.10 = f32[40,4,256]{2,1,0:T(4,128)} collective-permute-done((f32[40,4,256]{2,1,0:T(4,128)}, f32[40,4,256]{2,1,0:T(4,128)}, u32[]{:S(2)}, u32[]{:S(2)}) %collective-permute-start.10) | collective-permute-done | bytes 163872 | tf_op jit(solution)/shard_map/ppermute | solution.py:17
  72.8 1.7 %select_maximum_fusion.4 = f32[40,24,264]{2,1,0:T(8,128)S(1)} fusion(f32[40,4,256]{2,1,0:T(4,128)} %collective-permute-done.10, f32[40,4,256]{2,1,0:T(4,128)S(1)} %collective-permute-done.11, f32[4,16,256]{2,1,0:T(8,128)S(1)} %collective-permute-done.8, f32[32,16,256]{2,1,0:T(8,128)S(1)} %fusion.66, f32[4,16,256]{2,1,0:T(8,128)S(1)} %collective-permute-done.9), kind=kLoop, calls=%fused_computation.8 | loop fusion | flops 3041280 | bytes 1996800 | tf_op jit(solution)/shard_map/concatenate | solution.py:18
  75.6 2.0 %fusion.39 = f32[32,16,256]{2,1,0:T(8,128)S(1)} fusion(f32[32,16,256]{2,1,0:T(8,128)S(1)} %bitcast.59, f32[32,16,256]{2,1,0:T(8,128)S(1)} %copy-done.3, f32[32,16,256]{2,1,0:T(8,128)S(1)} %fusion.66, f32[4,16,256]{2,1,0:T(8,128)S(1)} %collective-permute-done.9, f32[4,16,256]{2,1,0:T(8,128)S(1)} %collective-permute-done.8, ...), kind=kLoop, calls=%fused_computation.116 | loop fusion | flops 6553600 | bytes 11141120 | tf_op jit(solution)/shard_map/add | solution.py:74
  77.7 4.4 %collective-permute-start.13 = (f32[4,16,256]{2,1,0:T(8,128)S(1)}, f32[4,16,256]{2,1,0:T(8,128)S(1)}, u32[]{:S(2)}, u32[]{:S(2)}) collective-permute-start(f32[4,16,256]{2,1,0:T(8,128)S(1)} %get-tuple-element.25), channel_id=1, source_target_pairs={{0,16},{1,17},{2,18},{3,19},{4,20},{5,21},{6,22},{7,23},{8,24},{9,... | collective-permute-start | bytes 196616 | tf_op jit(solution)/shard_map/ppermute | solution.py:14
  84.0 4.3 %collective-permute-done.12 = f32[4,16,256]{2,1,0:T(8,128)S(1)} collective-permute-done((f32[4,16,256]{2,1,0:T(8,128)S(1)}, f32[4,16,256]{2,1,0:T(8,128)S(1)}, u32[]{:S(2)}, u32[]{:S(2)}) %collective-permute-start.12) | collective-permute-done | bytes 65568 | tf_op jit(solution)/shard_map/ppermute | solution.py:17
  89.0 4.3 %collective-permute-start.15 = (f32[40,4,256]{2,1,0:T(4,128)}, f32[40,4,256]{2,1,0:T(4,128)S(1)}, u32[]{:S(2)}, u32[]{:S(2)}) collective-permute-start(f32[40,4,256]{2,1,0:T(4,128)} %get-tuple-element.11), channel_id=1, source_target_pairs={{0,4},{4,8},{8,12},{1,5},{5,9},{9,13},{2,6},{6,10},{10,14},{3,7},{... | collective-permute-start | bytes 491528 | tf_op jit(solution)/shard_map/ppermute | solution.py:14
  93.3 1.5 collective-permute-start.14
  95.8 1.9 %collective-permute-done.14 = f32[40,4,256]{2,1,0:T(4,128)} collective-permute-done((f32[40,4,256]{2,1,0:T(4,128)}, f32[40,4,256]{2,1,0:T(4,128)}, u32[]{:S(2)}, u32[]{:S(2)}) %collective-permute-start.14) | collective-permute-done | bytes 163872 | tf_op jit(solution)/shard_map/ppermute | solution.py:17
  97.7 1.7 %select_maximum_fusion = f32[40,24,264]{2,1,0:T(8,128)S(1)} fusion(f32[40,4,256]{2,1,0:T(4,128)} %collective-permute-done.14, f32[40,4,256]{2,1,0:T(4,128)S(1)} %collective-permute-done.15, f32[4,16,256]{2,1,0:T(8,128)S(1)} %collective-permute-done.12, f32[32,16,256]{2,1,0:T(8,128)S(1)} %fusion.39, f32[4,16,256]{2,1,0:T(8,128)S(1)} %collective-permute-done.13), kind=kLoop, calls=%fused_computation.4 | loop fusion | flops 3041280 | bytes 1996800 | tf_op jit(solution)/shard_map/concatenate | solution.py:18
  100.9 2.9 %fusion.149 = (f32[32,16,256]{2,1,0:T(8,128)S(1)}, f32[32,16,256]{2,1,0:T(8,128)}) fusion(f32[32,16,256]{2,1,0:T(8,128)S(1)} %fusion.39, f32[32,16,256]{2,1,0:T(8,128)S(1)} %fusion.66, f32[32,16,256]{2,1,0:T(8,128)S(1)} %fusion.93, bf16[1,4,32,16,256]{4,3,2,1,0:T(8,128)(2,1)S(1)} %copy-done.8, f32[32,16,256]{2,1,0:T(8,128)S(1)} %bitcast.56, ...), kind=kLoop, calls=%fused_computation.267 | loop fusion | flops 7995392 | bytes 13238272 | tf_op jit(solution)/shard_map/add | solution.py:79
  103.7 34.8 %reshape.77 = f32[16,2,8,2,128,2]{5,4,3,2,1,0:T(8,128)} reshape(f32[32,16,256]{2,1,0:T(8,128)S(1)} %get-tuple-element.3) | data formatting | bytes 1048576 | tf_op jit(solution)/shard_map/reshape | solution.py:49
  138.6 12.2 %reduce_sum.18 = f32[16,8,128]{2,1,0:T(8,128)S(1)} reduce(f32[16,2,8,2,128,2]{5,4,3,2,1,0:T(8,128)} %reshape.77, f32[]{:T(128)} %constant.9.clone.1), dimensions={1,3,5}, to_apply=%region_0.1 | reduce | flops 114688 | bytes 589828 | tf_op jit(solution)/shard_map/reduce_sum | solution.py:49
  150.8 14.8 %all-gather = f32[64,8,128]{2,1,0:T(8,128)S(1)} all-gather(f32[16,8,128]{2,1,0:T(8,128)S(1)} %broadcast_multiply_fusion), channel_id=2, replica_groups=mesh['gx'=2,'gy'=4,'shot'=4] {'shot'}, dimensions={0}, use_global_device_ids=true | all-gather | bytes 327680 | tf_op jit(solution)/shard_map/all_gather | solution.py:81
  (64 shorter events, 20.0 us)
Async XLA Ops:
  0.6 21.3 %copy-start = (bf16[1,1,64,16,256]{4,3,2,1,0:T(8,128)(2,1)S(1)}, bf16[1,1,64,16,256]{4,3,2,1,0:T(8,128)(2,1)}, u32[]{:S(2)}) copy-start(bf16[1,1,64,16,256]{4,3,2,1,0:T(8,128)(2,1)} %param.14) | copy-start | bytes 1572868
  0.6 21.6 %copy-start.10 = (s32[1,1,64]{2,1,0:T(1,128)S(1)}, s32[1,1,64]{2,1,0:T(1,128)}, u32[]{:S(2)}) copy-start(s32[1,1,64]{2,1,0:T(1,128)} %param.16) | copy-start | bytes 772
  1.6 22.5 %collective-permute-start = (f32[4,16,256]{2,1,0:T(8,128)S(1)}, f32[4,16,256]{2,1,0:T(8,128)S(1)}, u32[]{:S(2)}, u32[]{:S(2)}) collective-permute-start(f32[4,16,256]{2,1,0:T(8,128)S(1)} %get-tuple-element.31), channel_id=1, source_target_pairs={{16,0},{17,1},{18,2},{19,3},{20,4},{21,5},{22,6},{23,7},{24,8},{25... | collective-permute-start | bytes 196616 | tf_op jit(solution)/shard_map/ppermute | solution.py:17
  2.9 21.2 %collective-permute-start.1 = (f32[4,16,256]{2,1,0:T(8,128)S(1)}, f32[4,16,256]{2,1,0:T(8,128)S(1)}, u32[]{:S(2)}, u32[]{:S(2)}) collective-permute-start(f32[4,16,256]{2,1,0:T(8,128)S(1)} %get-tuple-element.32), channel_id=1, source_target_pairs={{0,16},{1,17},{2,18},{3,19},{4,20},{5,21},{6,22},{7,23},{8,24},{9,... | collective-permute-start | bytes 196616 | tf_op jit(solution)/shard_map/ppermute | solution.py:14
  21.9 2.2 %copy-start.1 = (f32[1,32,16,256]{3,2,1,0:T(8,128)S(1)}, f32[1,32,16,256]{3,2,1,0:T(8,128)}, u32[]{:S(2)}) copy-start(f32[1,32,16,256]{3,2,1,0:T(8,128)} %param.10) | copy-start | bytes 1572868
  24.2 4.9 %collective-permute-start.3 = (f32[40,4,256]{2,1,0:T(4,128)S(1)}, f32[40,4,256]{2,1,0:T(4,128)S(1)}, u32[]{:S(2)}, u32[]{:S(2)}) collective-permute-start(f32[40,4,256]{2,1,0:T(4,128)S(1)} %get-tuple-element.23), channel_id=1, source_target_pairs={{0,4},{4,8},{8,12},{1,5},{5,9},{9,13},{2,6},{6,10},{10,14},{3,7},{... | collective-permute-start | bytes 491528 | tf_op jit(solution)/shard_map/ppermute | solution.py:14
  26.5 3.3 %collective-permute-start.2 = (f32[40,4,256]{2,1,0:T(4,128)S(1)}, f32[40,4,256]{2,1,0:T(4,128)S(1)}, u32[]{:S(2)}, u32[]{:S(2)}) collective-permute-start(f32[40,4,256]{2,1,0:T(4,128)S(1)} %get-tuple-element.24), channel_id=1, source_target_pairs={{4,0},{8,4},{12,8},{5,1},{9,5},{13,9},{6,2},{10,6},{14,10},{7,3},{... | collective-permute-start | bytes 491528 | tf_op jit(solution)/shard_map/ppermute | solution.py:17
  30.5 1.0 copy-start.3
  30.5 1.2 copy-start.9
  33.7 14.1 %copy-start.7 = (f32[1,512,256]{1,2,0:T(8,128)S(1)}, f32[1,512,256]{1,2,0:T(8,128)}, u32[]{:S(2)}) copy-start(f32[1,512,256]{1,2,0:T(8,128)} %get-tuple-element.7) | copy-start | bytes 1572868
  33.8 6.3 %collective-permute-start.4 = (f32[4,16,256]{2,1,0:T(8,128)S(1)}, f32[4,16,256]{2,1,0:T(8,128)S(1)}, u32[]{:S(2)}, u32[]{:S(2)}) collective-permute-start(f32[4,16,256]{2,1,0:T(8,128)S(1)} %get-tuple-element.29), channel_id=1, source_target_pairs={{16,0},{17,1},{18,2},{19,3},{20,4},{21,5},{22,6},{23,7},{24,8},{25... | collective-permute-start | bytes 196616 | tf_op jit(solution)/shard_map/ppermute | solution.py:17
  35.2 6.4 %collective-permute-start.5 = (f32[4,16,256]{2,1,0:T(8,128)S(1)}, f32[4,16,256]{2,1,0:T(8,128)S(1)}, u32[]{:S(2)}, u32[]{:S(2)}) collective-permute-start(f32[4,16,256]{2,1,0:T(8,128)S(1)} %get-tuple-element.30), channel_id=1, source_target_pairs={{0,16},{1,17},{2,18},{3,19},{4,20},{5,21},{6,22},{7,23},{8,24},{9,... | collective-permute-start | bytes 196616 | tf_op jit(solution)/shard_map/ppermute | solution.py:14
  42.4 5.6 %collective-permute-start.7 = (f32[40,4,256]{2,1,0:T(4,128)}, f32[40,4,256]{2,1,0:T(4,128)S(1)}, u32[]{:S(2)}, u32[]{:S(2)}) collective-permute-start(f32[40,4,256]{2,1,0:T(4,128)} %get-tuple-element.19), channel_id=1, source_target_pairs={{0,4},{4,8},{8,12},{1,5},{5,9},{9,13},{2,6},{6,10},{10,14},{3,7},{... | collective-permute-start | bytes 491528 | tf_op jit(solution)/shard_map/ppermute | solution.py:14
  46.5 4.1 %collective-permute-start.6 = (f32[40,4,256]{2,1,0:T(4,128)}, f32[40,4,256]{2,1,0:T(4,128)}, u32[]{:S(2)}, u32[]{:S(2)}) collective-permute-start(f32[40,4,256]{2,1,0:T(4,128)} %get-tuple-element.20), channel_id=1, source_target_pairs={{4,0},{8,4},{12,8},{5,1},{9,5},{13,9},{6,2},{10,6},{14,10},{7,3},{... | collective-permute-start | bytes 491528 | tf_op jit(solution)/shard_map/ppermute | solution.py:17
  55.4 14.6 %copy-start.6 = (f32[1,512,256]{1,2,0:T(8,128)S(1)}, f32[1,512,256]{1,2,0:T(8,128)}, u32[]{:S(2)}) copy-start(f32[1,512,256]{1,2,0:T(8,128)} %get-tuple-element.6) | copy-start | bytes 1572868
  55.5 6.3 %collective-permute-start.8 = (f32[4,16,256]{2,1,0:T(8,128)S(1)}, f32[4,16,256]{2,1,0:T(8,128)S(1)}, u32[]{:S(2)}, u32[]{:S(2)}) collective-permute-start(f32[4,16,256]{2,1,0:T(8,128)S(1)} %get-tuple-element.27), channel_id=1, source_target_pairs={{16,0},{17,1},{18,2},{19,3},{20,4},{21,5},{22,6},{23,7},{24,8},{25... | collective-permute-start | bytes 196616 | tf_op jit(solution)/shard_map/ppermute | solution.py:17
  56.9 6.4 %collective-permute-start.9 = (f32[4,16,256]{2,1,0:T(8,128)S(1)}, f32[4,16,256]{2,1,0:T(8,128)S(1)}, u32[]{:S(2)}, u32[]{:S(2)}) collective-permute-start(f32[4,16,256]{2,1,0:T(8,128)S(1)} %get-tuple-element.28), channel_id=1, source_target_pairs={{0,16},{1,17},{2,18},{3,19},{4,20},{5,21},{6,22},{7,23},{8,24},{9,... | collective-permute-start | bytes 196616 | tf_op jit(solution)/shard_map/ppermute | solution.py:14
  64.1 6.1 %collective-permute-start.11 = (f32[40,4,256]{2,1,0:T(4,128)}, f32[40,4,256]{2,1,0:T(4,128)S(1)}, u32[]{:S(2)}, u32[]{:S(2)}) collective-permute-start(f32[40,4,256]{2,1,0:T(4,128)} %get-tuple-element.15), channel_id=1, source_target_pairs={{0,4},{4,8},{8,12},{1,5},{5,9},{9,13},{2,6},{6,10},{10,14},{3,7},{... | collective-permute-start | bytes 491528 | tf_op jit(solution)/shard_map/ppermute | solution.py:14
  68.7 4.1 %collective-permute-start.10 = (f32[40,4,256]{2,1,0:T(4,128)}, f32[40,4,256]{2,1,0:T(4,128)}, u32[]{:S(2)}, u32[]{:S(2)}) collective-permute-start(f32[40,4,256]{2,1,0:T(4,128)} %get-tuple-element.16), channel_id=1, source_target_pairs={{4,0},{8,4},{12,8},{5,1},{9,5},{13,9},{6,2},{10,6},{14,10},{7,3},{... | collective-permute-start | bytes 491528 | tf_op jit(solution)/shard_map/ppermute | solution.py:17
  77.6 23.0 %copy-start.2 = (f32[32,16,256]{2,1,0:T(8,128)}, f32[32,16,256]{2,1,0:T(8,128)S(1)}, u32[]{:S(2)}) copy-start(f32[32,16,256]{2,1,0:T(8,128)S(1)} %fusion.39) | copy-start | bytes 1572868
  77.6 17.2 %copy-start.5 = (f32[1,512,256]{1,2,0:T(8,128)S(1)}, f32[1,512,256]{1,2,0:T(8,128)}, u32[]{:S(2)}) copy-start(f32[1,512,256]{1,2,0:T(8,128)} %get-tuple-element.5) | copy-start | bytes 1572868
  77.7 6.3 %collective-permute-start.13 = (f32[4,16,256]{2,1,0:T(8,128)S(1)}, f32[4,16,256]{2,1,0:T(8,128)S(1)}, u32[]{:S(2)}, u32[]{:S(2)}) collective-permute-start(f32[4,16,256]{2,1,0:T(8,128)S(1)} %get-tuple-element.25), channel_id=1, source_target_pairs={{0,16},{1,17},{2,18},{3,19},{4,20},{5,21},{6,22},{7,23},{8,24},{9,... | collective-permute-start | bytes 196616 | tf_op jit(solution)/shard_map/ppermute | solution.py:14
  82.1 6.2 %collective-permute-start.12 = (f32[4,16,256]{2,1,0:T(8,128)S(1)}, f32[4,16,256]{2,1,0:T(8,128)S(1)}, u32[]{:S(2)}, u32[]{:S(2)}) collective-permute-start(f32[4,16,256]{2,1,0:T(8,128)S(1)} %get-tuple-element.26), channel_id=1, source_target_pairs={{16,0},{17,1},{18,2},{19,3},{20,4},{21,5},{22,6},{23,7},{24,8},{25... | collective-permute-start | bytes 196616 | tf_op jit(solution)/shard_map/ppermute | solution.py:17
  89.0 6.8 %collective-permute-start.15 = (f32[40,4,256]{2,1,0:T(4,128)}, f32[40,4,256]{2,1,0:T(4,128)S(1)}, u32[]{:S(2)}, u32[]{:S(2)}) collective-permute-start(f32[40,4,256]{2,1,0:T(4,128)} %get-tuple-element.11), channel_id=1, source_target_pairs={{0,4},{4,8},{8,12},{1,5},{5,9},{9,13},{2,6},{6,10},{10,14},{3,7},{... | collective-permute-start | bytes 491528 | tf_op jit(solution)/shard_map/ppermute | solution.py:14
  93.3 4.4 %collective-permute-start.14 = (f32[40,4,256]{2,1,0:T(4,128)}, f32[40,4,256]{2,1,0:T(4,128)}, u32[]{:S(2)}, u32[]{:S(2)}) collective-permute-start(f32[40,4,256]{2,1,0:T(4,128)} %get-tuple-element.12), channel_id=1, source_target_pairs={{4,0},{8,4},{12,8},{5,1},{9,5},{13,9},{6,2},{10,6},{14,10},{7,3},{... | collective-permute-start | bytes 491528 | tf_op jit(solution)/shard_map/ppermute | solution.py:17
  99.4 1.2 copy-start.4
  99.4 1.5 copy-start.8
